TPU v7x, 512 devices: a whole 4x4x16 slice. The times are simulated.
512 devices in a mesh: dp: 16 (over x, y), tm: 32 (over z, core).
Axes of the slice: x: 4, y: 4, z: 16, core: 2. Of those that a mesh axis runs over, the one named last changes fastest.
Arguments:
- records: bfloat16 [16, 4096, 1024], P('dp', 'tm'), may hold values from -6 to 6
- x_weight: bfloat16 [1024, 512], replicated, may hold values from -0.1875 to 0.1875
- bc_weight: bfloat16 [1024, 256], replicated, may hold values from -0.1875 to 0.1875
- decay_codes: int32 [16, 4096, 8], P('dp', 'tm'), may hold values from 0 to 524
- out_grad: bfloat16 [16, 4096, 512], P('dp', 'tm'), may hold values from -6 to 6
Outputs:
- y_out: bfloat16 [16, 4096, 512], P('dp', 'tm')
- x_grad: float32 [1024, 512], P('tm')
- bc_grad: float32 [1024, 256], P('tm')
All inputs are finite; a program needn't handle non-finite values.
Results may differ from a plain program's by a relative error of at most 0.0085.
Values sent between devices are 32-bit elements; how exact they have to be, the bound alone decides.
No kernel may reach another device: no remote copies, remote signals or barrier semaphores. Data moves between devices by JAX's collectives and lax.ppermute only.
A program may use at most 64 MiB of HBM per device.

v0:
```python
import jax
import jax.numpy as jnp
from jax import lax
from jax.sharding import PartitionSpec as P

SPAN = 128
highest = lax.Precision.HIGHEST


def entering(part, axis, combine, identity, reverse):
    count = lax.axis_size(axis)
    place = lax.axis_index(axis)
    ahead = count - 1 - place if reverse else place
    gathered = jax.tree.map(lambda a: lax.all_gather(a, axis), part)
    state = jax.tree.map(lambda a, e: jnp.zeros_like(a) + jnp.asarray(e, a.dtype), part, identity)

    def one(turn, state):
        source = count - 1 - turn if reverse else turn
        return combine(
            state, jax.tree.map(lambda a: lax.dynamic_index_in_dim(a, source, 0, False), gathered)
        )

    return lax.fori_loop(0, ahead, one, state)


def span_kernel(log_decay):
    running = jnp.cumsum(log_decay, axis=1)
    length = log_decay.shape[1]
    causal = lax.broadcasted_iota(jnp.int32, (length, length), 0) >= lax.broadcasted_iota(
        jnp.int32, (length, length), 1
    )
    causal = causal[None, None, :, :]
    heads_first = jnp.transpose(running, (0, 2, 1))
    gaps = heads_first[:, :, :, None] - heads_first[:, :, None, :]
    kernel = jnp.where(causal, jnp.exp(jnp.where(causal, gaps, 0.0)), 0.0)
    return (running, kernel)


def block_scores(readout, inject):
    return jnp.einsum(
        "rtn,rsn->rts",
        readout.astype(jnp.bfloat16),
        inject.astype(jnp.bfloat16),
        preferred_element_type=jnp.float32,
    )


def forward_span(carry_state, pieces):
    mixer_f, inject, readout, cot_heads, log_decay = pieces
    running, kernel = span_kernel(log_decay)
    scores = block_scores(readout, inject)
    mixing = kernel * scores[:, None, :, :]
    decayed = jnp.exp(running)
    within = jnp.einsum("rhts,rshp->rthp", mixing, mixer_f, precision=highest)
    carried = decayed[..., None] * jnp.einsum(
        "rhpn,rtn->rthp", carry_state, readout, precision=highest
    )
    pair_dots = jnp.einsum("rthp,rshp->rhts", cot_heads, mixer_f, precision=highest)
    grad_read = jnp.einsum("rhts,rsn->rtn", kernel * pair_dots, inject, precision=highest)
    grad_read = grad_read + jnp.einsum(
        "rthp,rhpn->rtn", decayed[..., None] * cot_heads, carry_state, precision=highest
    )
    to_end = jnp.exp(running[:, -1:, :] - running)
    new_state = jnp.exp(running[:, -1, :])[:, :, None, None] * carry_state
    new_state = new_state + jnp.einsum(
        "rshp,rsn->rhpn", to_end[..., None] * mixer_f, inject, precision=highest
    )
    return (new_state, (within + carried, grad_read))


def reverse_span(adjoint, pieces):
    mixer_f, inject, readout, cot_heads, log_decay = pieces
    running, kernel = span_kernel(log_decay)
    scores = block_scores(readout, inject)
    mixing = kernel * scores[:, None, :, :]
    pair_dots = jnp.einsum("rthp,rshp->rhts", cot_heads, mixer_f, precision=highest)
    to_end = jnp.exp(running[:, -1:, :] - running)
    grad_mixer = jnp.einsum("rhts,rthp->rshp", mixing, cot_heads, precision=highest)
    grad_mixer = grad_mixer + to_end[..., None] * jnp.einsum(
        "rhpn,rsn->rshp", adjoint, inject, precision=highest
    )
    grad_inject = jnp.einsum("rhts,rtn->rsn", kernel * pair_dots, readout, precision=highest)
    grad_inject = grad_inject + jnp.einsum(
        "rshp,rhpn->rsn", to_end[..., None] * mixer_f, adjoint, precision=highest
    )
    new_adjoint = jnp.exp(running[:, -1, :])[:, :, None, None] * adjoint
    new_adjoint = new_adjoint + jnp.einsum(
        "rthp,rtn->rhpn", jnp.exp(running)[..., None] * cot_heads, readout, precision=highest
    )
    return (new_adjoint, (grad_mixer, grad_inject))


def to_blocks(array, frames):
    return array.reshape((frames // SPAN, 1, SPAN) + array.shape[1:])


def combine_pair(earlier, later_one):
    return (earlier[0] * later_one[0], later_one[0][:, :, None, None] * earlier[1] + later_one[1])


def body(records, x_weight, bc_weight, decay_codes, out_grad):
    signal = records[0]
    codes = decay_codes[0]
    frames_dev, model_dim = signal.shape
    head_count = codes.shape[1]
    mixer_dim = x_weight.shape[1]
    head_size = mixer_dim // head_count
    state_size = bc_weight.shape[1] // 2
    tm_count = lax.axis_size("tm")
    groups = lax.axis_size("dp")
    out_scale = (state_size * frames_dev * tm_count) ** (-0.5)
    grad_scale = (groups * frames_dev * tm_count) ** (-0.5)
    decay_unit = 1.0 / (32.0 * frames_dev * tm_count)
    mixer_in = jnp.dot(signal, x_weight, preferred_element_type=jnp.float32).astype(jnp.bfloat16)
    state_proj = jnp.dot(signal, bc_weight, preferred_element_type=jnp.float32).astype(jnp.bfloat16)
    log_decay = -decay_unit * codes.astype(jnp.float32)
    cotangent = out_grad[0].astype(jnp.float32) * out_scale
    mixer_f = mixer_in.astype(jnp.float32).reshape(frames_dev, head_count, head_size)
    inject = state_proj[:, :state_size].astype(jnp.float32)
    readout = state_proj[:, state_size:].astype(jnp.float32)
    cot_heads = cotangent.reshape(frames_dev, head_count, head_size)
    blocks = (
        to_blocks(mixer_f, frames_dev),
        to_blocks(inject, frames_dev),
        to_blocks(readout, frames_dev),
        to_blocks(cot_heads, frames_dev),
        to_blocks(log_decay, frames_dev),
    )
    zero_state = jnp.zeros((1, head_count, head_size, state_size), jnp.float32)
    end_state, (local_out, local_read) = lax.scan(forward_span, zero_state, blocks)
    start_adjoint, (local_grad, local_inject) = lax.scan(
        reverse_span, zero_state, blocks, reverse=True
    )
    running = jnp.cumsum(log_decay, axis=0)
    device_log = running[-1]
    identity = (jnp.ones((1, head_count), jnp.float32), zero_state)
    carry_in = entering(
        (jnp.exp(device_log)[None], end_state), "tm", combine_pair, identity, False
    )[1][0]
    adjoint_in = entering(
        (jnp.exp(device_log)[None], start_adjoint), "tm", combine_pair, identity, True
    )[1][0]
    decayed = jnp.exp(running)
    to_end = jnp.exp(device_log[None] - running)
    output = local_out.reshape(frames_dev, head_count, head_size)
    output = output + decayed[..., None] * jnp.einsum(
        "hpn,tn->thp", carry_in, readout, precision=highest
    )
    grad_read = local_read.reshape(frames_dev, state_size)
    grad_read = grad_read + jnp.einsum(
        "thp,hpn->tn", decayed[..., None] * cot_heads, carry_in, precision=highest
    )
    grad_mixer = local_grad.reshape(frames_dev, head_count, head_size)
    grad_mixer = grad_mixer + to_end[..., None] * jnp.einsum(
        "hpn,tn->thp", adjoint_in, inject, precision=highest
    )
    grad_inject = local_inject.reshape(frames_dev, state_size)
    grad_inject = grad_inject + jnp.einsum(
        "thp,hpn->tn", to_end[..., None] * mixer_f, adjoint_in, precision=highest
    )
    grad_mix = grad_mixer.reshape(frames_dev, mixer_dim).astype(jnp.bfloat16)
    grad_proj = jnp.concatenate([grad_inject, grad_read], axis=1).astype(jnp.bfloat16)
    grad_cat = jnp.concatenate([grad_mix, grad_proj], axis=1)
    grad_share = lax.psum_scatter(
        lax.dot_general(
            signal, grad_cat, (((0,), (0,)), ((), ())), preferred_element_type=jnp.float32
        ),
        "tm",
        scatter_dimension=0,
        tiled=True,
    )
    grad_share = lax.psum(grad_share, "dp")
    grad_share = grad_share * grad_scale
    y_out = output.reshape(frames_dev, mixer_dim).astype(jnp.bfloat16)[None]
    return (y_out, grad_share[:, :mixer_dim], grad_share[:, mixer_dim:])


def solution(mesh):
    return jax.shard_map(
        body,
        mesh=mesh,
        in_specs=(P("dp", "tm", None), P(), P(), P("dp", "tm", None), P("dp", "tm", None)),
        out_specs=(P("dp", "tm", None), P("tm", None), P("tm", None)),
        check_vma=False,
    )
```

profile of v0, /device:TPU:32, one launch (start us, length us, event | category | flops | bytes accessed | tf_op | source)
XLA Modules:
  0.0 444.9 jit_solution(17753559127679987640)
XLA Ops:
  7.2 0.8 fusion.69
  9.1 1.4 convolution_convert_fusion.1
  10.5 1.3 convert_multiply_fusion
  11.9 1.0 convolution_add_fusion.1
  13.0 1.0 copy.79
  14.1 1.0 convolution_add_fusion
  15.5 33.9 %all-gather.3 = f32[32,1,8]{2,1,0:T(1,128)S(1)} all-gather(f32[1,1,8]{2,1,0:T(1,128)S(1)} %get-tuple-element.267), channel_id=2, replica_groups=mesh['dp'=16,'tm'=32] {'tm'}, dimensions={0}, use_global_device_ids=true | all-gather | bytes 1056 | tf_op jit(solution)/shard_map/all_gather | solution.py:14
  49.5 0.3 fusion.2
  49.8 0.4 convolution_bitcast_fusion.4
  50.2 0.4 convolution_bitcast_fusion.6
  50.6 0.7 fusion
  51.4 0.8 fusion.4
  52.1 44.4 %all-gather.7.cloned.1.call-done = f32[256,64,128]{2,1,0:T(8,128)} async-done(((f32[8,64,128]{2,1,0:T(8,128)}), f32[256,64,128]{2,1,0:T(8,128)}) %all-gather.7.cloned.1.call-update) | async-done | bytes 8388624 | tf_op jit(solution)/shard_map/all_gather | solution.py:14
  96.6 2.2 while.16
  96.6 1.1 bitcast_add_fusion.4
  97.7 1.1 bitcast_add_fusion.4
  98.8 76.1 %all-gather.9.cloned.1.call-done = f32[256,64,128]{2,1,0:T(8,128)} async-done(((f32[8,64,128]{2,1,0:T(8,128)}), f32[256,64,128]{2,1,0:T(8,128)}) %all-gather.9.cloned.1.call-update) | async-done | bytes 8388624 | tf_op jit(solution)/shard_map/all_gather | solution.py:14
  174.9 31.9 %while.17 = (s32[]{:T(128)}, f32[1,8,64,128]{3,2,1,0:T(8,128)S(1)}, s32[]{:T(128)}, f32[32,1,8]{2,1,0:T(1,128)S(1)}, f32[32,1,8,64,128]{4,3,2,1,0:T(8,128)}, /*index=5*/s32[]{:T(128)}, s32[]{:T(128)}, s32[]{:T(128)}, s32[]{:T(128)}) while((s32[]{:T(128)}, f32[1,8,64,128]{3,2,1,0:T(8,128)S(1)}, s32[]{:T(128)}, f32[32,1,8]{2,1,0:T(1,128)S(1)}, ...), condition=%wide.region_5.6_spmd, body=%wide.region_4.5_spmd.sunk | while | flops 131078 | bytes 786683 | solution.py:23
  174.9 1.1 bitcast_add_fusion.5
  176.0 1.1 bitcast_add_fusion.5
  177.1 1.1 bitcast_add_fusion.5
  178.2 1.1 bitcast_add_fusion.5
  179.3 1.1 bitcast_add_fusion.5
  180.4 1.1 bitcast_add_fusion.5
  181.5 1.1 bitcast_add_fusion.5
  182.6 1.1 bitcast_add_fusion.5
  183.7 1.1 bitcast_add_fusion.5
  184.8 1.1 bitcast_add_fusion.5
  185.9 1.1 bitcast_add_fusion.5
  187.0 1.1 bitcast_add_fusion.5
  188.1 1.1 bitcast_add_fusion.5
  189.2 1.1 bitcast_add_fusion.5
  190.4 1.1 bitcast_add_fusion.5
  191.5 1.1 bitcast_add_fusion.5
  192.6 1.1 bitcast_add_fusion.5
  193.7 1.1 bitcast_add_fusion.5
  194.8 1.1 bitcast_add_fusion.5
  195.9 1.1 bitcast_add_fusion.5
  197.0 1.1 bitcast_add_fusion.5
  198.1 1.1 bitcast_add_fusion.5
  199.2 1.1 bitcast_add_fusion.5
  200.3 1.1 bitcast_add_fusion.5
  201.4 1.1 bitcast_add_fusion.5
  202.5 1.1 bitcast_add_fusion.5
  203.6 1.1 bitcast_add_fusion.5
  204.7 1.1 bitcast_add_fusion.5
  205.8 1.1 bitcast_add_fusion.5
  206.8 0.6 convolution_bitcast_fusion.5
  207.4 0.3 fusion.10
  207.7 0.6 convolution_bitcast_fusion.3
  208.3 0.2 fusion.14
  208.6 0.2 fusion.13
  208.8 2.2 convolution_bitcast_fusion
  211.1 3.5 copy.87
  214.7 0.3 fusion.6
  214.9 0.7 fusion.8
  215.7 101.2 %reduce-scatter.4.cloned.1.call-done = f32[32,768]{1,0:T(8,128)} async-done(((f32[1024,768]{1,0:T(8,128)}), f32[32,768]{1,0:T(8,128)}) %reduce-scatter.4.cloned.1.call-update) | async-done | bytes 98320
  316.9 1.8 copy.88
  318.7 0.3 fusion.9
  319.0 0.8 copy.84
  319.7 116.2 %all-reduce.2.cloned.1.call-done = f32[32,768]{0,1:T(8,128)} async-done(((f32[32,768]{0,1:T(8,128)}), f32[32,768]{0,1:T(8,128)}) %all-reduce.2.cloned.1.call-update) | async-done | bytes 98320 | tf_op jit(solution)/shard_map/psum | solution.py:172
  435.9 1.0 broadcast_multiply_fusion
  437.0 0.7 copy.85
  437.7 0.7 copy.86
  (70 shorter events, 2.3 us)
Async XLA Ops:
  7.2 3.3 copy-start
  7.2 89.4 %all-gather.7.cloned.1.call-start = ((), (), s32[]{:S(2)}) async-start(), calls=%async_computation.2 | async-start | bytes 8650752 | tf_op jit(solution)/shard_map/all_gather | solution.py:14
  12.9 161.9 %all-gather.9.cloned.1.call-start = ((), (), s32[]{:S(2)}) async-start(), calls=%async_computation.3 | async-start | bytes 8650752 | tf_op jit(solution)/shard_map/all_gather | solution.py:14
  14.1 194.7 %copy-start.1 = (bf16[1,128,1024]{2,1,0:T(8,128)(2,1)S(1)}, bf16[1,128,1024]{2,1,0:T(8,128)(2,1)}, u32[]{:S(2)}) copy-start(bf16[1,128,1024]{2,1,0:T(8,128)(2,1)} %param.9) | copy-start | bytes 786436
  15.1 301.7 %reduce-scatter.4.cloned.1.call-start = ((), (), s32[]{:S(2)}) async-start(), calls=%async_computation.4 | async-start | bytes 3244032
  214.6 221.3 %all-reduce.2.cloned.1.call-start = ((), (), s32[]{:S(2)}) async-start(), calls=%async_computation.1 | async-start | bytes 786432 | tf_op jit(solution)/shard_map/psum | solution.py:172
Sparse Core Ops, SparseCore 0:
  13.0 83.4 all-gather.6
  98.7 76.1 all-gather.8
  214.7 102.0 reduce-scatter.3
  320.3 115.5 all-reduce.1
where the time goes:
time: 446 us; the launch traced here: 445 us
  waiting for transfers between devices  338 us (76%)
  other arithmetic  35.2 us (8%)
  blocking collectives  33.9 us (8%)
  between operations  14 us (3%)
  matrix products  12.6 us (3%)
  local copies, waits for them, and re-layouts  10 us (2%)
    all_gather x2, waiting for transfers between devices, entering(): gathered = jax.tree.map(lambda a: lax.all_gather(a, axis), part)  121 us
    psum x1, waiting for transfers between devices, body(): grad_share = lax.psum(grad_share, 'dp')  116 us
    unnamed x5, waiting for transfers between devices  101 us
    all_gather x1, blocking collectives, entering(): gathered = jax.tree.map(lambda a: lax.all_gather(a, axis), part)  33.9 us
    add x31, other arithmetic, combine_pair(): later_one[0][:, :, None, None] * earlier[1] + later_one[1]  32.9 us
  transfers between devices with their start and end apart: 4, of which 4 were waited for; matrix products, arithmetic and copies ran while one was open for 2% of the time, Pallas kernels for 0%

commit v1 on v0

--- a/solution.py
+++ b/solution.py
@@ -5,6 +5,12 @@
 
 SPAN = 128
 highest = lax.Precision.HIGHEST
+
+
+def summed_here(x, axis):
+    terms = lax.all_gather(x, axis, axis=0, tiled=False)
+    total = terms.sum(axis=0)
+    return total
 
 
 def entering(part, axis, combine, identity, reverse):
@@ -169,7 +175,7 @@
         scatter_dimension=0,
         tiled=True,
     )
-    grad_share = lax.psum(grad_share, "dp")
+    grad_share = summed_here(grad_share, "dp")
     grad_share = grad_share * grad_scale
     y_out = output.reshape(frames_dev, mixer_dim).astype(jnp.bfloat16)[None]
     return (y_out, grad_share[:, :mixer_dim], grad_share[:, mixer_dim:])

time: 446 us -> 391 us (0.88)
  the two profiles are of different devices: /device:TPU:32 before, /device:TPU:1 now
where the time goes in v1:
time: 391 us; the launch traced here: 390 us
  waiting for transfers between devices  281 us (72%)
  blocking collectives  37.4 us (10%)
  other arithmetic  35.7 us (9%)
  between operations  14 us (4%)
  matrix products  12.6 us (3%)
  local copies, waits for them, and re-layouts  7.99 us (2%)
    all_gather x2, waiting for transfers between devices, entering(): gathered = jax.tree.map(lambda a: lax.all_gather(a, axis), part)  120 us
    reduce_scatter x1, waiting for transfers between devices, body(): lax.psum_scatter(lax.dot_general(signal, grad_cat, (((0,), (0,)), ((), ()...  101 us
    all_gather x1, waiting for transfers between devices, summed_here(): terms = lax.all_gather(x, axis, axis=0, tiled=False)  59.9 us
    all_gather x1, blocking collectives, entering(): gathered = jax.tree.map(lambda a: lax.all_gather(a, axis), part)  37.4 us
    add x31, other arithmetic, combine_pair(): later_one[0][:, :, None, None] * earlier[1] + later_one[1]  32.9 us
  transfers between devices with their start and end apart: 4, of which 4 were waited for; matrix products, arithmetic and copies ran while one was open for 2% of the time, Pallas kernels for 0%

profile of v1, /device:TPU:1, one launch (start us, length us, event | category | flops | bytes accessed | tf_op | source)
XLA Modules:
  0.0 389.6 jit_solution(6191505337869478765)
XLA Ops:
  7.2 0.8 fusion.69
  8.1 0.2 reduce_window_sum.27
  9.1 1.4 convolution_convert_fusion.1
  10.5 1.3 convert_multiply_fusion
  11.9 1.0 convolution_add_fusion.1
  13.0 1.0 copy.75
  14.1 1.0 convolution_add_fusion
  15.5 37.4 %all-gather.4 = f32[32,1,8]{2,1,0:T(1,128)S(1)} all-gather(f32[1,1,8]{2,1,0:T(1,128)S(1)} %get-tuple-element.267), channel_id=2, replica_groups=mesh['dp'=16,'tm'=32] {'tm'}, dimensions={0}, use_global_device_ids=true | all-gather | bytes 1056 | tf_op jit(solution)/shard_map/all_gather | solution.py:20
  52.9 0.3 fusion.2
  53.2 0.4 convolution_bitcast_fusion.4
  53.6 0.4 convolution_bitcast_fusion.6
  54.0 0.7 fusion
  54.8 0.8 fusion.4
  55.5 42.9 %all-gather.9.cloned.1.call-done = f32[256,64,128]{2,1,0:T(8,128)} async-done(((f32[8,64,128]{2,1,0:T(8,128)}), f32[256,64,128]{2,1,0:T(8,128)}) %all-gather.9.cloned.1.call-update) | async-done | bytes 8388624 | tf_op jit(solution)/shard_map/all_gather | solution.py:20
  98.4 1.1 while.16
  98.5 1.1 bitcast_add_fusion.4
  99.5 77.1 %all-gather.11.cloned.1.call-done = f32[256,64,128]{2,1,0:T(8,128)} async-done(((f32[8,64,128]{2,1,0:T(8,128)}), f32[256,64,128]{2,1,0:T(8,128)}) %all-gather.11.cloned.1.call-update) | async-done | bytes 8388624 | tf_op jit(solution)/shard_map/all_gather | solution.py:20
  176.6 33.0 %while.17 = (s32[]{:T(128)}, f32[1,8,64,128]{3,2,1,0:T(8,128)S(1)}, s32[]{:T(128)}, f32[32,1,8]{2,1,0:T(1,128)S(1)}, f32[32,1,8,64,128]{4,3,2,1,0:T(8,128)}, /*index=5*/s32[]{:T(128)}, s32[]{:T(128)}, s32[]{:T(128)}, s32[]{:T(128)}) while((s32[]{:T(128)}, f32[1,8,64,128]{3,2,1,0:T(8,128)S(1)}, s32[]{:T(128)}, f32[32,1,8]{2,1,0:T(1,128)S(1)}, ...), condition=%wide.region_5.6_spmd, body=%wide.region_4.5_spmd.sunk | while | flops 131078 | bytes 786683 | solution.py:29
  176.7 1.1 bitcast_add_fusion.5
  177.8 1.1 bitcast_add_fusion.5
  178.9 1.1 bitcast_add_fusion.5
  180.0 1.1 bitcast_add_fusion.5
  181.1 1.1 bitcast_add_fusion.5
  182.2 1.1 bitcast_add_fusion.5
  183.3 1.1 bitcast_add_fusion.5
  184.4 1.1 bitcast_add_fusion.5
  185.5 1.1 bitcast_add_fusion.5
  186.6 1.1 bitcast_add_fusion.5
  187.7 1.1 bitcast_add_fusion.5
  188.8 1.1 bitcast_add_fusion.5
  189.9 1.1 bitcast_add_fusion.5
  191.0 1.1 bitcast_add_fusion.5
  192.1 1.1 bitcast_add_fusion.5
  193.2 1.1 bitcast_add_fusion.5
  194.3 1.1 bitcast_add_fusion.5
  195.4 1.1 bitcast_add_fusion.5
  196.5 1.1 bitcast_add_fusion.5
  197.6 1.1 bitcast_add_fusion.5
  198.7 1.1 bitcast_add_fusion.5
  199.8 1.1 bitcast_add_fusion.5
  200.9 1.1 bitcast_add_fusion.5
  202.0 1.1 bitcast_add_fusion.5
  203.1 1.1 bitcast_add_fusion.5
  204.2 1.1 bitcast_add_fusion.5
  205.3 1.1 bitcast_add_fusion.5
  206.4 1.1 bitcast_add_fusion.5
  207.5 1.1 bitcast_add_fusion.5
  208.6 1.1 bitcast_add_fusion.5
  209.7 0.6 convolution_bitcast_fusion.5
  210.3 0.3 fusion.10
  210.6 0.6 convolution_bitcast_fusion.3
  211.2 0.2 fusion.14
  211.4 0.2 fusion.13
  211.7 2.2 convolution_bitcast_fusion
  213.9 3.5 copy.82
  217.5 100.7 %reduce-scatter.4.cloned.1.call-done = f32[32,768]{1,0:T(8,128)} async-done(((f32[1024,768]{1,0:T(8,128)}), f32[32,768]{1,0:T(8,128)}) %reduce-scatter.4.cloned.1.call-update) | async-done | bytes 98320 | tf_op jit(solution)/shard_map/reduce_scatter | solution.py:170
  318.3 0.3 fusion.6
  318.6 0.7 fusion.8
  319.3 0.3 fusion.9
  319.6 0.8 copy.81
  320.4 59.9 %all-gather.13.cloned.1.call-done = f32[512,768]{1,0:T(8,128)} async-done(((f32[32,768]{1,0:T(8,128)}), f32[512,768]{1,0:T(8,128)}) %all-gather.13.cloned.1.call-update) | async-done | bytes 1572880 | tf_op jit(solution)/shard_map/all_gather | solution.py:11
  380.3 1.5 reduce_sum.25
  381.8 0.6 slice.33
  382.4 0.6 slice.34
  (68 shorter events, 2.1 us)
Async XLA Ops:
  7.2 3.3 copy-start
  7.2 91.2 %all-gather.9.cloned.1.call-start = ((), (), s32[]{:S(2)}) async-start(), calls=%async_computation.1 | async-start | bytes 8650752 | tf_op jit(solution)/shard_map/all_gather | solution.py:20
  12.9 163.7 %all-gather.11.cloned.1.call-start = ((), (), s32[]{:S(2)}) async-start(), calls=%async_computation.2 | async-start | bytes 8650752 | tf_op jit(solution)/shard_map/all_gather | solution.py:20
  14.1 197.6 %copy-start.1 = (bf16[1,128,1024]{2,1,0:T(8,128)(2,1)S(1)}, bf16[1,128,1024]{2,1,0:T(8,128)(2,1)}, u32[]{:S(2)}) copy-start(bf16[1,128,1024]{2,1,0:T(8,128)(2,1)} %param.9) | copy-start | bytes 786436
  15.1 303.1 %reduce-scatter.4.cloned.1.call-start = ((), (), s32[]{:S(2)}) async-start(), calls=%async_computation.4 | async-start | bytes 3244032 | tf_op jit(solution)/shard_map/reduce_scatter | solution.py:170
  217.5 162.8 %all-gather.13.cloned.1.call-start = ((), (), s32[]{:S(2)}) async-start(), calls=%async_computation.3 | async-start | bytes 1671168 | tf_op jit(solution)/shard_map/all_gather | solution.py:11
Sparse Core Ops, SparseCore 0:
  13.0 85.3 all-gather.8
  100.5 76.0 all-gather.10
  217.6 100.6 reduce-scatter.3
  321.6 58.6 all-gather.12
